TPU v7x, 128 devices: a whole 4x4x4 slice. The times are simulated.
128 devices in a mesh: row: 8 (over y_lo, x), col: 16 (over y_hi, z, core).
Axes of the slice: x: 4, y: 4 (y_hi: 2, y_lo: 2; y = y_hi * 2 + y_lo), z: 4, core: 2. Of those that a mesh axis runs over, the one named last changes fastest.
Arguments:
- sign_iterate: bfloat16 [8192, 8192], P('row', 'col'), may hold values from -6 to 6
- sign_square: bfloat16 [8192, 8192], P('row', 'col'), may hold values from -0.125 to 0.125
- pattern_x: int32 [64, 64], P('row', 'col'), may hold values 0 or 1
- pattern_y: int32 [64, 64], P('row', 'col'), may hold values 0 or 1
- pattern_product: int32 [64, 64], P('row', 'col'), may hold values 0 or 1
- orbital_energy: bfloat16 [8192], P('row'), may hold values from -3 to 1
- pair_dest: int32 [128, 128, 1], P(('row', 'col')), may hold values from 0 to 127; in each aligned block of 128 rows (0 to 127, 128 to 255, ..., all dimensions but the last counted through in order) at most 2 rows name the same one
- pair_block: int32 [128, 128], P(('row', 'col')), may hold values from 0 to 31
- force_h: bfloat16 [32768, 128, 128], P(('row', 'col')), may hold values from -0.5 to 0.5
- force_s: bfloat16 [32768, 128, 128], P(('row', 'col')), may hold values from -0.5 to 0.5
Outputs:
- sign_next: bfloat16 [8192, 8192], P('row', 'col')
- forces: float32 [32768], P(('row', 'col'))
Inputs may be any that keep to these rules, and one draw needn't show every extreme that they name: `pair_dest`: among the 128 entries of one device no owner is named more than 2 times, a bound that some block reaches. `pair_block`: A row-major index into the device's own 8 x 4 grid of blocks.
All inputs are finite; a program needn't handle non-finite values. No bound on the sum of `pattern_x` or of `pattern_y` or of `pattern_product` on one device may be relied on, other than what follows from the above.
Results may differ from a plain program's by a relative error of at most 0.003.
Values may be sent and summed in bfloat16 or wider, within the bound.
No kernel may reach another device: no remote copies, remote signals or barrier semaphores. Data moves between devices by JAX's collectives and lax.ppermute only.
A program may use at most 128 MiB of HBM per device.

v0:
```python
import jax
import jax.numpy as jnp
from jax import lax
from jax.sharding import PartitionSpec as P

BS = 128
QB = 4
CAP = 2


def masked_tile(tile, pattern):
    rows, cols = tile.shape
    shaped = tile.reshape(rows // BS, BS, cols // BS, BS) * pattern[:, None, :, None].astype(
        tile.dtype
    )
    return shaped.reshape(rows, cols)


def tile_blocks(tile):
    rows, cols = tile.shape
    shaped = tile.reshape(rows // BS, BS, cols // BS, BS).transpose(0, 2, 1, 3)
    return shaped.reshape(rows // BS * (cols // BS), BS * BS)


def rank_within(dest):
    entries = dest.shape[-1]
    order = jnp.arange(entries, dtype=jnp.int32)
    same = (dest[..., :, None] == dest[..., None, :]) & (order[None, :] < order[:, None])
    return jnp.sum(same.astype(jnp.int32), axis=-1)


def shards(
    sign_iterate,
    sign_square,
    pattern_x,
    pattern_y,
    pattern_product,
    orbital_energy,
    pair_dest,
    pair_block,
    force_h,
    force_s,
):
    rows_x, cols_x = sign_iterate.shape
    xmask = masked_tile(sign_iterate, pattern_x)
    ymask = masked_tile(sign_square, pattern_y)
    y_whole = lax.all_gather(ymask, "row", axis=0, tiled=True)
    product = jnp.dot(
        lax.all_gather(xmask, "col", axis=1, tiled=True),
        y_whole,
        preferred_element_type=jnp.float32,
    )
    product = masked_tile(product, pattern_product)
    xnew = 1.5 * xmask.astype(jnp.float32) - 0.5 * product
    sign_next = xnew.astype(jnp.bfloat16)
    global_rows = lax.axis_index("row") * rows_x + jnp.arange(rows_x, dtype=jnp.int32)
    global_cols = lax.axis_index("col") * cols_x + jnp.arange(cols_x, dtype=jnp.int32)
    identity = (global_rows[:, None] == global_cols[None, :]).astype(jnp.float32)
    density = (0.5 * identity - 0.5 * xnew).astype(jnp.bfloat16)
    dens_blocks = tile_blocks(density)
    n_rows = lax.axis_size("row")
    n_cols = lax.axis_size("col")
    devices = n_rows * n_cols
    slots = devices * CAP
    local_rows = rows_x // BS
    dest = pair_dest[0, :, 0]
    wanted = pair_block[0]
    rank = rank_within(dest)
    slot = dest * CAP + rank
    pick_slot = (jnp.arange(slots, dtype=jnp.int32)[:, None] == slot[None, :]).astype(jnp.bfloat16)
    pick_block = (
        wanted[:, None] == jnp.arange(dens_blocks.shape[0], dtype=jnp.int32)[None, :]
    ).astype(jnp.bfloat16)
    routing_table = jnp.dot(pick_slot, pick_block, preferred_element_type=jnp.float32).astype(
        jnp.bfloat16
    )
    send_dens = jnp.dot(routing_table, dens_blocks, preferred_element_type=jnp.float32).astype(
        jnp.bfloat16
    )
    pick_row = ((wanted // QB)[:, None] == jnp.arange(local_rows, dtype=jnp.int32)[None, :]).astype(
        jnp.bfloat16
    )
    slot_rows = jnp.dot(pick_slot, pick_row, preferred_element_type=jnp.float32).astype(
        jnp.bfloat16
    )
    send_energy = jnp.dot(
        slot_rows, orbital_energy.reshape(local_rows, BS), preferred_element_type=jnp.float32
    ).astype(jnp.bfloat16)
    payload = jnp.concatenate([send_dens.reshape(slots, BS, BS), send_energy[:, None, :]], axis=1)
    height = BS + 1
    received = lax.all_to_all(
        payload.reshape(devices, CAP, height * BS),
        ("row", "col"),
        split_axis=0,
        concat_axis=0,
        tiled=True,
    )
    received = received.reshape(slots, height, BS)
    recv_dens = received[:, :BS, :]
    energies = received[:, BS, :].astype(jnp.float32)
    h_term = jnp.einsum("sab,sab->s", recv_dens, force_h, preferred_element_type=jnp.float32)
    s_rows = jnp.einsum("sab,sab->sa", recv_dens, force_s, preferred_element_type=jnp.float32)
    forces = h_term - jnp.sum(energies * s_rows, axis=1)
    return (sign_next, forces)


def solution(mesh):
    in_specs = (
        P("row", "col"),
        P("row", "col"),
        P("row", "col"),
        P("row", "col"),
        P("row", "col"),
        P("row"),
        P(("row", "col"), None, None),
        P(("row", "col"), None),
        P(("row", "col"), None, None),
        P(("row", "col"), None, None),
    )
    out_specs = (P("row", "col"), P(("row", "col")))
    return jax.shard_map(shards, mesh=mesh, in_specs=in_specs, out_specs=out_specs, check_vma=False)
```

profile of v0, /device:TPU:6, one launch (start us, length us, event | category | flops | bytes accessed | tf_op | source)
XLA Modules:
  0.0 425.4 jit_solution(5564351684399702492)
XLA Ops:
  7.2 0.0 all-gather.5.cloned.1.call-start
  7.3 0.7 convert_element_type.48
  7.9 0.1 copy.22
  8.0 0.3 mul.72
  8.4 2.4 bitcast_multiply_fusion.1
  10.8 0.0 all-gather.5.cloned.1.call-update
  10.8 0.0 all-gather.3.cloned.1.call-start
  10.9 0.7 convert_element_type.46
  11.6 0.1 copy.21
  11.7 0.3 mul.67
  12.0 2.3 bitcast_multiply_fusion.2
  14.3 0.0 all-gather.3.cloned.1.call-update
  14.4 0.1 copy.23
  14.5 0.2 convert_reduce_fusion
  14.7 0.5 fusion.5
  15.2 0.1 copy.25
  15.3 87.7 %all-gather.5.cloned.1.call-done = bf16[8192,512]{1,0:T(8,128)(2,1)} async-done(((bf16[1024,512]{1,0:T(8,128)(2,1)}), bf16[8192,512]{1,0:T(8,128)(2,1)}) %all-gather.5.cloned.1.call-update) | async-done | bytes 8388624 | tf_op jit(solution)/shard_map/all_gather | solution.py:47
  103.0 123.0 %all-gather.3.cloned.1.call-done = bf16[1024,8192]{1,0:T(8,128)(2,1)} async-done(((bf16[1024,512]{1,0:T(8,128)(2,1)}), bf16[1024,8192]{1,0:T(8,128)(2,1)}) %all-gather.3.cloned.1.call-update) | async-done | bytes 16777232 | tf_op jit(solution)/shard_map/all_gather | solution.py:49
  226.0 0.3 mul.75
  226.3 16.1 %subtract_convert_fusion = (bf16[1024,512]{1,0:T(8,128)(2,1)S(1)}, bf16[1024,512]{1,0:T(8,128)(2,1)}) fusion(s32[512]{0:T(512)S(1)} %iota_add_fusion.1, s32[1024]{0:T(1024)S(1)} %iota_add_fusion, f32[128,8,4,128]{3,2,1,0:T(4,128)S(1)} %bitcast.41, bf16[1024,8192]{1,0:T(8,128)(2,1)} %all-gather.3.cloned.1.call-done, ...), kind=kOutput, calls=%fused_computation.10 | convolution fusion | flops 8595701760 | bytes 30414848 | tf_op jit(solution)/shard_map/dot_general | solution.py:48
  242.4 0.3 reshape.86
  242.7 0.2 copy.24
  243.0 5.2 %fusion.2 = bf16[32,8,128,128]{3,1,2,0:T(8,128)(2,1)} fusion(bf16[4,8,128,128]{3,2,1,0:T(8,128)(2,1)S(1)} %bitcast.38, s32[128]{0:T(128)S(1)} %get-tuple-element.8, s32[128]{0:T(128)S(1)} %bitcast.43), kind=kOutput, calls=%fused_computation.6 | convolution fusion | flops 274771968 | bytes 9438208 | tf_op jit(solution)/shard_map/dot_general | solution.py:77
  248.2 9.2 %copy.40 = bf16[32,8,128,128]{3,2,1,0:T(8,128)(2,1)} copy(bf16[32,8,128,128]{3,1,2,0:T(8,128)(2,1)} %fusion.2) | data formatting | bytes 16777216
  257.4 9.0 %pad_maximum_fusion = bf16[256,129,128]{2,1,0:T(8,128)(2,1)} fusion(bf16[256,1,128]{2,1,0:T(2,128)(2,1)S(1)} %copy.25, bf16[256,128,128]{2,1,0:T(8,128)(2,1)} %bitcast.37), kind=kLoop, calls=%fused_computation.5 | loop fusion | flops 16908288 | bytes 16908288 | tf_op jit(solution)/shard_map/concatenate | solution.py:89
  266.4 13.2 %reshape.90 = bf16[128,2,16512]{2,1,0:T(2,128)(2,1)} reshape(bf16[256,129,128]{2,1,0:T(8,128)(2,1)} %pad_maximum_fusion) | data formatting | bytes 16908288 | tf_op jit(solution)/shard_map/reshape | solution.py:92
  279.6 111.1 %all_to_all.5 = bf16[128,2,16512]{2,1,0:T(2,128)(2,1)} all-to-all(bf16[128,2,16512]{2,1,0:T(2,128)(2,1)} %reshape.90), channel_id=1, replica_groups=mesh['row'=8,'col'=16] {'row','col'}, dimensions={0} | all-to-all | bytes 16908288 | tf_op jit(solution)/shard_map/all_to_all | solution.py:91
  390.7 14.2 %reshape.91 = bf16[256,129,128]{2,1,0:T(8,128)(2,1)} reshape(bf16[128,2,16512]{2,1,0:T(2,128)(2,1)} %all_to_all.5) | data formatting | bytes 16908288 | tf_op jit(solution)/shard_map/reshape | solution.py:98
  404.9 1.1 slice_convert_fusion
  406.0 11.8 %fusion.1 = (f32[256,128]{1,0:T(8,128)S(1)}, f32[256]{0:T(256)S(1)}) fusion(bf16[256,128,128]{2,1,0:T(8,128)(2,1)} %param.19, bf16[256,129,128]{2,1,0:T(8,128)(2,1)} %reshape.91, bf16[256,128,128]{2,1,0:T(8,128)(2,1)} %param.18), kind=kLoop, calls=%fused_computation.4 | loop fusion | flops 29327104 | bytes 25297920 | tf_op jit(solution)/shard_map/sab,sab->sa/dot_general | solution.py:102
  417.8 0.1 multiply_reduce_fusion
  417.9 0.6 sub.18
  (14 shorter events, 0.0 us)
Async XLA Ops:
  7.2 7.5 %copy-start = (bf16[1024]{0:T(1024)(128)(2,1)S(1)}, bf16[1024]{0:T(1024)(128)(2,1)}, u32[]{:S(2)}) copy-start(bf16[1024]{0:T(1024)(128)(2,1)} %param.15) | copy-start | bytes 6148
  7.2 7.2 %copy-start.3 = (s32[8,4]{0,1:T(4,128)S(1)}, s32[8,4]{0,1:T(4,128)}, u32[]{:S(2)}) copy-start(s32[8,4]{0,1:T(4,128)} %param.14) | copy-start | bytes 388
  7.2 7.3 %copy-start.4 = (s32[1,128,1]{1,2,0:T(1,128)S(1)}, s32[1,128,1]{1,2,0:T(1,128)}, u32[]{:S(2)}) copy-start(s32[1,128,1]{1,2,0:T(1,128)} %param.16) | copy-start | bytes 1540
  7.2 7.5 %copy-start.2 = (s32[1,128]{1,0:T(1,128)S(1)}, s32[1,128]{1,0:T(1,128)}, u32[]{:S(2)}) copy-start(s32[1,128]{1,0:T(1,128)} %param.17) | copy-start | bytes 1540
  7.2 95.8 %all-gather.5.cloned.1.call-start = ((), (), s32[]{:S(2)}) async-start(), calls=%async_computation.2 | async-start | bytes 9437184 | tf_op jit(solution)/shard_map/all_gather | solution.py:47
  10.8 215.1 %all-gather.3.cloned.1.call-start = ((), (), s32[]{:S(2)}) async-start(), calls=%async_computation.1 | async-start | bytes 17825792 | tf_op jit(solution)/shard_map/all_gather | solution.py:49
  404.9 13.7 %copy-start.1 = (bf16[1024]{0:T(1024)(128)(2,1)S(1)}, bf16[1024]{0:T(1024)(128)(2,1)}, u32[]{:S(2)}) copy-start(bf16[1024]{0:T(1024)(128)(2,1)} %param.15) | copy-start | bytes 6148
Sparse Core Ops, SparseCore 0:
  11.0 92.0 all-gather.4
  105.8 120.0 all-gather.2
where the time goes:
time: 426 us; the launch traced here: 425 us
  waiting for transfers between devices  211 us (50%)
  blocking collectives  111 us (26%)
  local copies, waits for them, and re-layouts  38.6 us (9%)
  other arithmetic  28.9 us (7%)
  matrix products  21.8 us (5%)
  between operations  14.2 us (3%)
    all_gather x1, waiting for transfers between devices, shards(): lax.all_gather(xmask, 'col', axis=1, tiled=True)  123 us
    all_to_all x1, blocking collectives, shards(): lax.all_to_all(payload.reshape(devices, CAP, height * BS), ('row', 'col')...  111 us
    all_gather x1, waiting for transfers between devices, shards(): y_whole = lax.all_gather(ymask, 'row', axis=0, tiled=True)  87.7 us
    dot_general x1, matrix products, shards(): jnp.dot(lax.all_gather(xmask, 'col', axis=1, tiled=True), y_whole, prefer...  16.1 us
    reshape x1, local copies, waits for them, and re-layouts, shards(): received = received.reshape(slots, height, BS)  14.2 us
    reshape x1, local copies, waits for them, and re-layouts, shards(): payload.reshape(devices, CAP, height * BS)  13.2 us
    dot_general x1, other arithmetic, shards(): jnp.einsum('sab,sab->sa', recv_dens, force_s, preferred_element_type=jnp....  11.8 us
    unnamed x11, local copies, waits for them, and re-layouts  9.24 us
  transfers between devices with their start and end apart: 2, of which 2 were waited for; matrix products, arithmetic and copies ran while one was open for 1% of the time, Pallas kernels for 0%

commit v1 on v0

--- a/solution.py
+++ b/solution.py
@@ -6,6 +6,9 @@
 BS = 128
 QB = 4
 CAP = 2
+ratios_fit = lambda a0: jnp.concatenate(
+    lax.all_to_all(jnp.stack([a0] * lax.axis_size("col"), axis=0), "col", 0, 0), axis=1
+)
 
 
 def masked_tile(tile, pattern):
@@ -45,11 +48,7 @@
     xmask = masked_tile(sign_iterate, pattern_x)
     ymask = masked_tile(sign_square, pattern_y)
     y_whole = lax.all_gather(ymask, "row", axis=0, tiled=True)
-    product = jnp.dot(
-        lax.all_gather(xmask, "col", axis=1, tiled=True),
-        y_whole,
-        preferred_element_type=jnp.float32,
-    )
+    product = jnp.dot(ratios_fit(xmask), y_whole, preferred_element_type=jnp.float32)
     product = masked_tile(product, pattern_product)
     xnew = 1.5 * xmask.astype(jnp.float32) - 0.5 * product
     sign_next = xnew.astype(jnp.bfloat16)

time: 426 us -> 626 us (1.47)
  the two profiles are of different devices: /device:TPU:6 before, /device:TPU:23 now
where the time goes in v1:
time: 626 us; the launch traced here: 624 us
  waiting for transfers between devices  428 us (68%)
  local copies, waits for them, and re-layouts  106 us (17%)
  starting transfers between devices  29.5 us (5%)
  other arithmetic  26.4 us (4%)
  matrix products  20.2 us (3%)
  between operations  14.3 us (2%)
    all_to_all x1, waiting for transfers between devices, lax.all_to_all(jnp.stack([a0] * lax.axis_size('col'), axis=0), 'col', 0, 0)  220 us
    all_to_all x1, waiting for transfers between devices, shards(): lax.all_to_all(payload.reshape(devices, CAP, height * BS), ('row', 'col')...  117 us
    all_gather x1, waiting for transfers between devices, shards(): y_whole = lax.all_gather(ymask, 'row', axis=0, tiled=True)  90.7 us
    dot_general x2, local copies, waits for them, and re-layouts, shards(): jnp.dot(ratios_fit(xmask), y_whole, preferred_element_type=jnp.float32)  37.6 us
    all_to_all x1, starting transfers between devices, shards(): lax.all_to_all(payload.reshape(devices, CAP, height * BS), ('row', 'col')...  20.7 us
    reshape x1, local copies, waits for them, and re-layouts, jnp.concatenate(lax.all_to_all(jnp.stack([a0] * lax.axis_size('col'), axi...  18.4 us
    dot_general x1, matrix products, shards(): jnp.dot(ratios_fit(xmask), y_whole, preferred_element_type=jnp.float32)  14.5 us
    reshape x1, local copies, waits for them, and re-layouts, shards(): received = received.reshape(slots, height, BS)  14.2 us
  transfers between devices with their start and end apart: 3, of which 3 were waited for; matrix products, arithmetic and copies ran while one was open for 3% of the time, Pallas kernels for 0%

profile of v1, /device:TPU:23, one launch (start us, length us, event | category | flops | bytes accessed | tf_op | source)
XLA Modules:
  0.0 623.9 jit_solution(11308408525288781365)
XLA Ops:
  7.2 0.7 convert_element_type.46
  7.9 1.5 copy.36
  9.4 0.2 mul.69
  9.6 0.1 bitcast_multiply_fusion.1
  9.7 0.5 copy.37
  10.3 6.0 stack.3
  16.3 8.8 %all-to-all-start = ((bf16[16,1024,512]{2,1,0:T(8,128)(2,1)}), bf16[16,1024,512]{2,1,0:T(8,128)(2,1)}, u32[]{:S(2)}, u32[]{:S(2)}) async-start(bf16[16,1024,512]{2,1,0:T(8,128)(2,1)} %stack.3), calls=%async_computation | async-start | bytes 33554432 | tf_op jit(solution)/shard_map/all_to_all | solution.py:10
  25.2 0.3 mul.74
  25.5 1.1 bitcast_multiply_fusion
  26.8 0.2 convert_reduce_fusion
  27.0 0.5 fusion.8
  27.6 90.7 %all-gather.2.cloned.1.call-done = bf16[8192,512]{1,0:T(8,128)(2,1)} async-done(((bf16[1024,512]{1,0:T(8,128)(2,1)}), bf16[8192,512]{1,0:T(8,128)(2,1)}) %all-gather.2.cloned.1.call-update) | async-done | bytes 8388624 | tf_op jit(solution)/shard_map/all_gather | solution.py:50
  118.3 12.0 %copy.40 = bf16[512,8192]{1,0:T(8,128)(2,1)} copy(bf16[512,8192]{0,1:T(8,128)(2,1)} %bitcast.59) | data formatting | bytes 16777216 | tf_op jit(solution)/shard_map/dot_general | solution.py:51
  130.3 220.1 %all-to-all-done = bf16[16,1024,512]{2,1,0:T(8,128)(2,1)} async-done(((bf16[16,1024,512]{2,1,0:T(8,128)(2,1)}), bf16[16,1024,512]{2,1,0:T(8,128)(2,1)}, u32[]{:S(2)}, u32[]{:S(2)}) %all-to-all-start) | async-done | bytes 16777248 | tf_op jit(solution)/shard_map/all_to_all | solution.py:10
  350.4 18.4 %copy.38 = bf16[1024,16,512]{2,1,0:T(8,128)(2,1)} copy(bf16[1024,16,512]{2,0,1:T(8,128)(2,1)} %bitcast) | data formatting | bytes 33554432 | tf_op jit(solution)/shard_map/reshape | solution.py:9
  368.9 25.6 %reshape.106 = bf16[8,128,8192,1]{2,1,0,3:T(8,128)(2,1)} reshape(bf16[1024,16,512]{2,1,0:T(8,128)(2,1)} %copy.38) | data formatting | bytes 33554432 | tf_op jit(solution)/shard_map/dot_general | solution.py:51
  394.5 14.5 %multiply_multiply_fusion = f32[8,128,4,128]{3,1,2,0:T(8,128)} fusion(bf16[4,128,8192,1]{2,1,0,3:T(8,128)(2,1)} %bitcast.60, bf16[8,128,8192,1]{2,1,0,3:T(8,128)(2,1)} %reshape.106, f32[8,4]{1,0:T(8,128)S(1)} %copy.41), kind=kOutput, calls=%fused_computation.11 | convolution fusion | flops 8590983168 | bytes 27263104 | tf_op jit(solution)/shard_map/dot_general | solution.py:51
  409.0 2.0 copy.42
  411.1 1.6 fusion.9
  412.7 0.3 copy.60
  413.0 0.8 copy.43
  413.8 5.2 fusion.4
  419.0 9.2 %copy.62 = bf16[32,8,128,128]{3,2,1,0:T(8,128)(2,1)} copy(bf16[32,8,128,128]{3,1,2,0:T(8,128)(2,1)} %fusion.4) | data formatting | bytes 16777216
  428.2 9.0 %pad_maximum_fusion = bf16[256,129,128]{2,1,0:T(8,128)(2,1)} fusion(bf16[256,1,128]{2,1,0:T(2,128)(2,1)S(1)} %copy.44, bf16[256,128,128]{2,1,0:T(8,128)(2,1)} %bitcast.58), kind=kLoop, calls=%fused_computation.7 | loop fusion | flops 16908288 | bytes 16908288 | tf_op jit(solution)/shard_map/concatenate | solution.py:88
  437.2 13.2 %reshape.103 = bf16[128,2,16512]{2,1,0:T(2,128)(2,1)} reshape(bf16[256,129,128]{2,1,0:T(8,128)(2,1)} %pad_maximum_fusion) | data formatting | bytes 16908288 | tf_op jit(solution)/shard_map/reshape | solution.py:91
  450.4 20.7 %all-to-all-start.1 = ((bf16[128,2,16512]{2,1,0:T(2,128)(2,1)}), bf16[128,2,16512]{2,1,0:T(2,128)(2,1)}, u32[]{:S(2)}, u32[]{:S(2)}) async-start(bf16[128,2,16512]{2,1,0:T(2,128)(2,1)} %reshape.103), calls=%async_computation.1 | async-start | bytes 16908288 | tf_op jit(solution)/shard_map/all_to_all | solution.py:90
  471.1 1.3 copy.45
  472.4 116.7 %all-to-all-done.1 = bf16[128,2,16512]{2,1,0:T(2,128)(2,1)} async-done(((bf16[128,2,16512]{2,1,0:T(2,128)(2,1)}), bf16[128,2,16512]{2,1,0:T(2,128)(2,1)}, u32[]{:S(2)}, u32[]{:S(2)}) %all-to-all-start.1) | async-done | bytes 8454176 | tf_op jit(solution)/shard_map/all_to_all | solution.py:90
  589.2 14.2 %reshape.104 = bf16[256,129,128]{2,1,0:T(8,128)(2,1)} reshape(bf16[128,2,16512]{2,1,0:T(2,128)(2,1)} %all-to-all-done.1) | data formatting | bytes 16908288 | tf_op jit(solution)/shard_map/reshape | solution.py:97
  603.4 1.1 slice_convert_fusion
  604.5 11.8 %fusion.1 = (f32[256,128]{1,0:T(8,128)S(1)}, f32[256]{0:T(256)S(1)}) fusion(bf16[256,128,128]{2,1,0:T(8,128)(2,1)} %param.19, bf16[256,129,128]{2,1,0:T(8,128)(2,1)} %reshape.104, bf16[256,128,128]{2,1,0:T(8,128)(2,1)} %param.18), kind=kLoop, calls=%fused_computation.4 | loop fusion | flops 29327104 | bytes 25297920 | tf_op jit(solution)/shard_map/sab,sab->sa/dot_general | solution.py:101
  616.5 0.6 sub.18
  (27 shorter events, 0.5 us)
Async XLA Ops:
  7.2 19.8 %copy-start = (bf16[1024]{0:T(1024)(128)(2,1)S(1)}, bf16[1024]{0:T(1024)(128)(2,1)}, u32[]{:S(2)}) copy-start(bf16[1024]{0:T(1024)(128)(2,1)} %param.15) | copy-start | bytes 6148
  16.2 8.8 %copy-start.5 = (s32[8,4]{0,1:T(4,128)S(1)}, s32[8,4]{0,1:T(4,128)}, u32[]{:S(2)}) copy-start(s32[8,4]{0,1:T(4,128)} %param.13) | copy-start | bytes 388
  16.2 9.3 %copy-start.3 = (bf16[1024,512]{1,0:T(8,128)(2,1)S(1)}, bf16[1024,512]{1,0:T(8,128)(2,1)}, u32[]{:S(2)}) copy-start(bf16[1024,512]{1,0:T(8,128)(2,1)} %param.11) | copy-start | bytes 3145732
  16.2 10.5 %copy-start.6 = (s32[8,4]{0,1:T(4,128)S(1)}, s32[8,4]{0,1:T(4,128)}, u32[]{:S(2)}) copy-start(s32[8,4]{0,1:T(4,128)} %param.14) | copy-start | bytes 388
  16.2 10.6 %copy-start.7 = (s32[1,128,1]{1,2,0:T(1,128)S(1)}, s32[1,128,1]{1,2,0:T(1,128)}, u32[]{:S(2)}) copy-start(s32[1,128,1]{1,2,0:T(1,128)} %param.16) | copy-start | bytes 1540
  16.2 10.7 %copy-start.4 = (s32[1,128]{1,0:T(1,128)S(1)}, s32[1,128]{1,0:T(1,128)}, u32[]{:S(2)}) copy-start(s32[1,128]{1,0:T(1,128)} %param.17) | copy-start | bytes 1540
  16.3 334.2 %all-to-all-start = ((bf16[16,1024,512]{2,1,0:T(8,128)(2,1)}), bf16[16,1024,512]{2,1,0:T(8,128)(2,1)}, u32[]{:S(2)}, u32[]{:S(2)}) async-start(bf16[16,1024,512]{2,1,0:T(8,128)(2,1)} %stack.3), calls=%async_computation | async-start | bytes 33554432 | tf_op jit(solution)/shard_map/all_to_all | solution.py:10
  25.0 93.3 %all-gather.2.cloned.1.call-start = ((), (), s32[]{:S(2)}) async-start(), calls=%async_computation.2 | async-start | bytes 9437184 | tf_op jit(solution)/shard_map/all_gather | solution.py:50
  450.4 20.7 %copy-start.2 = (bf16[1024,512]{0,1:T(8,128)(2,1)S(1)}, bf16[1024,512]{0,1:T(8,128)(2,1)}, u32[]{:S(2)}) copy-start(bf16[1024,512]{0,1:T(8,128)(2,1)} %get-tuple-element.11) | copy-start | bytes 3145732
  450.4 138.8 %all-to-all-start.1 = ((bf16[128,2,16512]{2,1,0:T(2,128)(2,1)}), bf16[128,2,16512]{2,1,0:T(2,128)(2,1)}, u32[]{:S(2)}, u32[]{:S(2)}) async-start(bf16[128,2,16512]{2,1,0:T(2,128)(2,1)} %reshape.103), calls=%async_computation.1 | async-start | bytes 16908288 | tf_op jit(solution)/shard_map/all_to_all | solution.py:90
  603.4 13.7 %copy-start.1 = (bf16[1024]{0:T(1024)(128)(2,1)S(1)}, bf16[1024]{0:T(1024)(128)(2,1)}, u32[]{:S(2)}) copy-start(bf16[1024]{0:T(1024)(128)(2,1)} %param.15) | copy-start | bytes 6148
Sparse Core Ops, SparseCore 0:
  28.1 90.1 all-gather.1
